TPU v7x, 256 devices: a whole 4x4x8 slice. The times are simulated.
256 devices in a mesh: seq: 32 (over y_lo, z, core), tp: 8 (over x, y_hi).
Axes of the slice: x: 4, y: 4 (y_hi: 2, y_lo: 2; y = y_hi * 2 + y_lo), z: 8, core: 2. Of those that a mesh axis runs over, the one named last changes fastest.
Arguments:
- query: bfloat16 [6144, 5120], P('seq', 'tp')
- span_keys: bfloat16 [6144, 5120], P('seq', 'tp'), may hold values from -6 to 6
- span_values: bfloat16 [6144, 5120], P('seq', 'tp'), may hold values from -48 to 48
- cache_keys: bfloat16 [8, 8192, 5120], P(None, 'seq', 'tp'), may hold values from -6 to 6
- cache_values: bfloat16 [8, 8192, 5120], P(None, 'seq', 'tp'), may hold values from -48 to 48
- out_weight: bfloat16 [5120, 5120], P('tp'), may hold values from -0.078125 to 0.078125
- cache_lengths: int32 [8], replicated, may hold values from 1 to 8192, as said below
- sink_counts: int32 [8], replicated, may hold values from 1 to 256, as said below
- windows: int32 [8], replicated, may hold values from 2048 to 4096, as said below
- block_of_slot: int32 [8, 32], replicated, may hold values from 0 to 31, each once within a row
Outputs:
- projected: bfloat16 [6144, 5120], P('seq', 'tp')
Inputs may be any that keep to these rules, and one draw needn't show every extreme that they name: `cache_lengths`: at least 1 and at most 8192; some request has exactly 8192. `sink_counts`: some request has exactly 256. `windows`: some request has exactly 4096. `block_of_slot`: each row is a permutation of 0 to 31.
All inputs are finite; a program needn't handle non-finite values.
Results may differ from a plain program's by a relative error of at most 0.015.
Values may be sent and summed in bfloat16 or wider, within the bound.
A program may use at most 192 MiB of HBM per device.

v0:
```python
import math

import jax
import jax.numpy as jnp
import numpy as np
from jax import lax
from jax.experimental import pallas as pl
from jax.experimental.pallas import tpu as pltpu
from jax.sharding import Mesh
from jax.sharding import PartitionSpec as P

HEAD = 128


NEG = -1e30


def attend(q_rows, chunks, span_k, span_v, params, places, interpret=False):
    total_rows, width = q_rows.shape
    rows = total_rows // places
    heads = width // HEAD
    n = len(chunks)
    cdev = chunks[0].shape[1]
    srows = span_k.shape[0]
    scale = 1.0 / math.sqrt(HEAD)

    def kernel(par, q_ref, *refs):
        kv_refs = refs[:n]
        sk_ref, sv_ref, o_ref, m_ref, l_ref = refs[n:]
        length = par[n + 1]
        window = par[n + 2]
        sinks = par[n + 3]
        row = lax.broadcasted_iota(jnp.int32, (total_rows, 1), 0)
        qpos = row % rows
        for j in range(places):
            qpos = jnp.where(row // rows == j, qpos + par[n + 4 + j], qpos)
        rows_here = total_rows
        q = q_ref[...]
        m = jnp.full((rows_here, 1), NEG, jnp.float32)
        l = jnp.zeros((rows_here, 1), jnp.float32)
        acc = jnp.zeros((rows_here, HEAD), jnp.float32)
        for c in range(n + 1):
            if c < n:
                keys = kv_refs[c][0]
                vals = kv_refs[c][1]
                kpos = par[c] + lax.broadcasted_iota(jnp.int32, (1, cdev), 1)
                valid = kpos < length
            else:
                keys = sk_ref[...]
                vals = sv_ref[...]
                kpos = par[n] + lax.broadcasted_iota(jnp.int32, (1, srows), 1)
                valid = kpos >= 0
            s = lax.dot_general(q, keys, (((1,), (1,)), ((), ())), preferred_element_type=jnp.float32) * scale
            mask = (kpos <= qpos) & ((qpos - kpos < window) | (kpos < sinks)) & valid
            s = jnp.where(mask, s, NEG)
            m_new = jnp.maximum(m, jnp.max(s, axis=1, keepdims=True))
            alpha = jnp.exp(m - m_new)
            p = jnp.exp(s - jnp.where(m_new > NEG, m_new, 0.0))
            l = alpha * l + jnp.sum(p, axis=1, keepdims=True)
            acc = alpha * acc + jnp.dot(p.astype(jnp.bfloat16), vals, preferred_element_type=jnp.float32)
            m = m_new
        o_ref[...] = acc.astype(o_ref.dtype)
        m_ref[...] = m
        l_ref[...] = l

    in_specs = [pl.BlockSpec((total_rows, HEAD), lambda h, par: (0, h))]
    in_specs += [pl.BlockSpec((2, cdev, HEAD), lambda h, par: (0, 0, h)) for _ in range(n)]
    in_specs += [pl.BlockSpec((srows, HEAD), lambda h, par: (0, h))] * 2
    out_specs = [
        pl.BlockSpec((total_rows, HEAD), lambda h, par: (0, h)),
        pl.BlockSpec((None, total_rows, 1), lambda h, par: (h, 0, 0)),
        pl.BlockSpec((None, total_rows, 1), lambda h, par: (h, 0, 0)),
    ]
    out_shape = [
        jax.ShapeDtypeStruct((total_rows, width), jnp.bfloat16),
        jax.ShapeDtypeStruct((heads, total_rows, 1), jnp.float32),
        jax.ShapeDtypeStruct((heads, total_rows, 1), jnp.float32),
    ]
    return pl.pallas_call(
        kernel,
        grid_spec=pltpu.PrefetchScalarGridSpec(
            num_scalar_prefetch=1, grid=(heads,), in_specs=in_specs, out_specs=out_specs
        ),
        out_shape=out_shape,
        interpret=interpret,
    )(params, q_rows, *chunks, span_k, span_v)


def layer(
    query,
    span_keys,
    span_values,
    cache_keys,
    cache_values,
    out_weight,
    cache_lengths,
    sink_counts,
    windows,
    block_of_slot,
):
    rows, width = query.shape
    heads_here = width // HEAD
    places = lax.axis_size("place")
    group = lax.axis_size("req")
    devices = places * group
    place = lax.axis_index("place")
    mine = lax.axis_index("req")
    me = place * group + mine
    cache_dev = cache_keys.shape[1]
    length = cache_lengths[mine]
    window = windows[mine]
    sinks = sink_counts[mine]
    seq = ("place", "req")

    ring = devices // 4
    core, z, y = me % 2, (me // 2) % ring, me // (2 * ring)

    def at(yy, zz, cc):
        return (yy * ring + zz % ring) * 2 + cc

    def request_of(index):
        return index % group

    moves = [(d, flip) for d in (-1, 0, 1) for flip in (0, 1)] + [("far", c) for c in (0, 1)]
    got_kv, got_slot = [], []
    for d, flip in moves:
        if d == "far":
            target = jnp.where(core == 0, at(y, z + 2, flip), at(y, z - 2, 1 - flip))
            source = jnp.where(core == flip, at(y, z - 2, 0), at(y, z + 2, 1))
            pairs = []
            for s_idx in range(devices):
                sc, sz, sy = s_idx % 2, (s_idx // 2) % ring, s_idx // (2 * ring)
                if sc == 0:
                    pairs.append((s_idx, (sy * ring + (sz + 2) % ring) * 2 + flip))
                else:
                    pairs.append((s_idx, (sy * ring + (sz - 2) % ring) * 2 + 1 - flip))
        else:
            target = at(y, z + d, core ^ flip)
            source = at(y, z - d, core ^ flip)
            pairs = []
            for s_idx in range(devices):
                sc, sz, sy = s_idx % 2, (s_idx // 2) % ring, s_idx // (2 * ring)
                pairs.append((s_idx, (sy * ring + (sz + d) % ring) * 2 + (sc ^ flip)))
        sent = request_of(target)
        chunk = jnp.stack(
            [
                lax.dynamic_index_in_dim(cache_keys, sent, 0, keepdims=False),
                lax.dynamic_index_in_dim(cache_values, sent, 0, keepdims=False),
            ]
        )
        if d != 0 or flip != 0:
            chunk = lax.ppermute(chunk, seq, pairs)
        got_kv.append(chunk)
        got_slot.append(source)

    span_q = [query]
    for k in range(1, places):
        pairs = [(p * group + i, ((p + k) % places) * group + i) for p in range(places) for i in range(group)]
        span_q.append(lax.ppermute(query, seq, pairs))
    span_q = jnp.stack(span_q)
    from_place = (place - jnp.arange(places, dtype=jnp.int32)) % places

    slots = jnp.stack(got_slot)
    blocks = block_of_slot[mine][slots]
    head_params = jnp.concatenate(
        [blocks * cache_dev, jnp.stack([length + place * rows, length, window, sinks])]
    )
    first_rows = length + from_place * rows

    def partial(picked):
        params = jnp.concatenate([head_params, first_rows[picked[0] : picked[-1] + 1]]).astype(jnp.int32)
        q_rows = span_q[picked[0] : picked[-1] + 1].reshape(-1, width)
        out, top, total = attend(q_rows, got_kv, span_keys, span_values, params, len(picked))
        stats = jnp.concatenate([top[..., 0].T, total[..., 0].T], axis=1)
        return out.reshape(len(picked), rows, width), stats.reshape(len(picked), rows, 2 * heads_here)

    other_sum, other_stats = partial(list(range(1, places)))
    own_sum, own_stats = partial([0])
    back_sum, back_stats = [own_sum[0]], [own_stats[0]]
    for k in range(1, places):
        pairs = [(p * group + i, ((p - k) % places) * group + i) for p in range(places) for i in range(group)]
        got = lax.ppermute((other_sum[k - 1], other_stats[k - 1]), seq, pairs)
        back_sum.append(got[0])
        back_stats.append(got[1])
    summed = jnp.stack(back_sum).astype(jnp.float32).reshape(places, rows, heads_here, HEAD)
    stats = jnp.stack(back_stats)
    top, total = stats[..., :heads_here], stats[..., heads_here:]
    best = jnp.max(top, axis=0)
    factor = jnp.exp(top - best[None])
    total = jnp.sum(total * factor, axis=0)
    summed = jnp.sum(summed * factor[..., None], axis=0)
    attention = (summed / total[..., None]).astype(jnp.bfloat16).reshape(rows, width)
    parts = lax.axis_size("tp")
    terms = jnp.einsum(
        "qf,fkc->kqc", attention, out_weight.reshape(width, parts, -1), preferred_element_type=jnp.float32
    )
    terms = lax.all_to_all(terms.astype(jnp.bfloat16), "tp", split_axis=0, concat_axis=0, tiled=True)
    return jnp.sum(terms.astype(jnp.float32), axis=0).astype(jnp.bfloat16)


def solution(mesh):
    seq_size = mesh.shape["seq"]
    requests = 8
    grid = Mesh(
        np.asarray(mesh.devices).reshape(seq_size // requests, requests, mesh.shape["tp"]),
        ("place", "req", "tp"),
    )
    seq = ("place", "req")
    return jax.shard_map(
        layer,
        mesh=grid,
        in_specs=(
            P(seq, "tp"),
            P(seq, "tp"),
            P(seq, "tp"),
            P(None, seq, "tp"),
            P(None, seq, "tp"),
            P("tp", None),
            P(),
            P(),
            P(),
            P(),
        ),
        out_specs=P(seq, "tp"),
        check_vma=False,
    )
```

profile of v0, /device:TPU:8, one launch (start us, length us, event | category | flops | bytes accessed | tf_op | source)
XLA Modules:
  0.0 198.7 jit_solution(3416016818243767241)
XLA Ops:
  0.0 7.2 %collective-permute-start.7 = (bf16[192,640]{1,0:T(8,128)(2,1)}, bf16[192,640]{1,0:T(8,128)(2,1)S(1)}, u32[]{:S(2)}, u32[]{:S(2)}) collective-permute-start(bf16[192,640]{1,0:T(8,128)(2,1)} %q_ref.1), channel_id=1, source_target_pairs={{0,64},{8,72},{16,80},{24,88},{32,96},{40,104},{48,112},{56,120},{... | collective-permute-start | bytes 737288 | tf_op jit(solution)/shard_map/ppermute | solution.py:159
  7.2 0.4 collective-permute-start.8
  7.6 1.4 collective-permute-start.9
  9.0 3.8 %constant_dynamic-slice_fusion = (bf16[1,256,640]{2,1,0:T(8,128)(2,1)S(1)}, bf16[1,256,640]{2,1,0:T(8,128)(2,1)S(1)}, bf16[1,256,640]{2,1,0:T(8,128)(2,1)S(1)}, ...) fusion(bf16[8,256,640]{2,1,0:T(8,128)(2,1)} %param.14, ...), kind=kLoop, calls=%fused_computation.29 | loop fusion | bytes 10485792 | tf_op jit(solution)/shard_map/jit(dynamic_index_in_dim)/dynamic_slice | solution.py:148
  12.8 0.9 pad_maximum_fusion.7
  13.7 1.6 collective-permute-start.5
  15.3 0.9 pad_maximum_fusion.8
  16.2 0.9 pad_maximum_fusion.6
  17.1 0.9 pad_maximum_fusion.5
  18.0 0.9 pad_maximum_fusion.4
  18.9 0.6 dynamic_slice.62
  19.5 0.9 pad_maximum_fusion.2
  20.4 0.9 pad_maximum_fusion.1
  21.4 0.6 fusion.9
  22.5 0.6 dynamic_slice.63
  23.2 0.6 dynamic_slice.64
  24.0 3.1 %collective-permute-start.4 = (bf16[2,256,640]{2,1,0:T(8,128)(2,1)}, bf16[2,256,640]{2,1,0:T(8,128)(2,1)S(1)}, u32[]{:S(2)}, u32[]{:S(2)}) collective-permute-start(bf16[2,256,640]{2,1,0:T(8,128)(2,1)} %pad_maximum_fusion.6), channel_id=1, source_target_pairs={{0,24},{8,16},{16,40},{24,32},{32,56},{40,48},{48,72},{56,64},{64,... | collective-permute-start | bytes 1966088 | tf_op jit(solution)/shard_map/ppermute | solution.py:152
  27.2 0.5 copy-done.7
  27.8 0.2 collective-permute-start.2
  28.0 20.7 %collective-permute-done.5.refs_6_ = bf16[2,256,640]{2,1,0:T(8,128)(2,1)S(1)} collective-permute-done((bf16[2,256,640]{2,1,0:T(8,128)(2,1)}, bf16[2,256,640]{2,1,0:T(8,128)(2,1)S(1)}, u32[]{:S(2)}, u32[]{:S(2)}) %collective-permute-start.5) | collective-permute-done | bytes 655392 | tf_op jit(solution)/shard_map/ppermute | solution.py:152
  48.7 21.1 %collective-permute-done.6.refs_7_ = bf16[2,256,640]{2,1,0:T(8,128)(2,1)S(1)} collective-permute-done((bf16[2,256,640]{2,1,0:T(8,128)(2,1)}, bf16[2,256,640]{2,1,0:T(8,128)(2,1)S(1)}, u32[]{:S(2)}, u32[]{:S(2)}) %collective-permute-start.6) | collective-permute-done | bytes 655392 | tf_op jit(solution)/shard_map/ppermute | solution.py:152
  69.9 0.6 gather_fusion
  70.5 2.4 %concatenate.35.par = s32[13]{0:T(128)} concatenate(s32[8]{0:T(128)S(1)} %broadcast_multiply_fusion, s32[1]{0:T(128)} %bitcast.11, s32[1]{0:T(128)} %dynamic_slice.62, s32[1]{0:T(128)} %dynamic_slice.63, s32[1]{0:T(128)} %dynamic_slice.64, s32[1]{0:T(128)S(1)} %bitcast.59), dimensions={0} | concatenate | bytes 104 | tf_op jit(solution)/shard_map/concatenate | solution.py:171
  73.0 2.4 %concatenate.36.par = s32[15]{0:T(128)} concatenate(s32[8]{0:T(128)S(1)} %broadcast_multiply_fusion, s32[1]{0:T(128)} %bitcast.11, s32[1]{0:T(128)} %dynamic_slice.62, s32[1]{0:T(128)} %dynamic_slice.63, s32[1]{0:T(128)} %dynamic_slice.64, s32[3]{0:T(128)S(1)} %slice.37), dimensions={0} | concatenate | bytes 120 | tf_op jit(solution)/shard_map/concatenate | solution.py:171
  75.4 2.0 pad_maximum_fusion.3.refs_2_
  77.4 2.0 %pad_maximum_fusion = bf16[3,192,640]{2,1,0:T(8,128)(2,1)} fusion(bf16[1,192,640]{2,1,0:T(8,128)(2,1)} %bitcast.15, bf16[1,192,640]{2,1,0:T(8,128)(2,1)} %bitcast.51, bf16[1,192,640]{2,1,0:T(8,128)(2,1)S(1)} %bitcast.50), kind=kLoop, calls=%fused_computation.6 | loop fusion | flops 737280 | bytes 1474560 | tf_op jit(solution)/shard_map/stack | solution.py:160
  79.4 5.2 %collective-permute-done.3.refs_4_ = bf16[2,256,640]{2,1,0:T(8,128)(2,1)S(1)} collective-permute-done((bf16[2,256,640]{2,1,0:T(8,128)(2,1)}, bf16[2,256,640]{2,1,0:T(8,128)(2,1)S(1)}, u32[]{:S(2)}, u32[]{:S(2)}) %collective-permute-start.3) | collective-permute-done | bytes 655392 | tf_op jit(solution)/shard_map/ppermute | solution.py:152
  84.7 1.5 collective-permute-done.refs_0_
  86.2 10.2 %shard_map.100 = (bf16[192,640]{1,0:T(8,128)(2,1)}, f32[5,192,1]{2,1,0:T(8,128)}, f32[5,192,1]{2,1,0:T(8,128)}) custom-call(s32[13]{0:T(128)} %concatenate.35.par, bf16[192,640]{1,0:T(8,128)(2,1)} %q_ref.1, bf16[2,256,640]{2,1,0:T(8,128)(2,1)} %collective-permute-done.refs_0_, bf16[2,256,640]{2,1,0:T(8,128)(2,1)} %collective-permute-done.1.refs_1_, ...), custom_call_target="tpu_custom_call" | custom-call | tf_op jit(solution)/shard_map/pallas_call | solution.py:79
  96.4 1.3 reduce.1
  97.7 1.3 reduce.2
  98.9 21.0 %shard_map.101 = (bf16[576,640]{1,0:T(8,128)(2,1)}, f32[5,576,1]{2,1,0:T(8,128)}, f32[5,576,1]{2,1,0:T(8,128)}) custom-call(s32[15]{0:T(128)} %concatenate.36.par, bf16[576,640]{1,0:T(8,128)(2,1)} %bitcast.44, bf16[2,256,640]{2,1,0:T(8,128)(2,1)} %collective-permute-done.refs_0_, bf16[2,256,640]{2,1,0:T(8,128)(2,1)} %collective-permute-done.1.refs_1_, ...), custom_call_target="tpu_custom_call" | custom-call | tf_op jit(solution)/shard_map/pallas_call | solution.py:79
  119.9 2.0 reduce.3
  121.9 1.9 reduce.4
  123.8 6.6 %collective-permute-start.13 = (f32[192,10]{0,1:T(8,128)S(1)}, f32[192,10]{0,1:T(8,128)S(1)}, u32[]{:S(2)}, u32[]{:S(2)}) collective-permute-start(f32[192,10]{0,1:T(8,128)S(1)} %get-tuple-element.38), channel_id=1, source_target_pairs={{0,192},{8,200},{16,208},{24,216},{32,224},{40,232},{48,240},{56,2... | collective-permute-start | bytes 23048 | tf_op jit(solution)/shard_map/ppermute | solution.py:182
  130.5 1.7 collective-permute-start.14
  132.4 6.9 %collective-permute-start.10 = (bf16[192,640]{1,0:T(8,128)(2,1)S(1)}, bf16[192,640]{1,0:T(8,128)(2,1)S(1)}, u32[]{:S(2)}, u32[]{:S(2)}) collective-permute-start(bf16[192,640]{1,0:T(8,128)(2,1)S(1)} %get-tuple-element.35), channel_id=1, source_target_pairs={{0,192},{8,200},{16,208},{24,216},{32,224},{40,232},{48,240},{56,2... | collective-permute-start | bytes 737288 | tf_op jit(solution)/shard_map/ppermute | solution.py:182
  139.3 0.4 collective-permute-start.11
  139.7 0.6 collective-permute-start.12
  140.3 0.6 collective-permute-done.15
  140.9 14.8 %collective-permute-done.10 = bf16[192,640]{1,0:T(8,128)(2,1)S(1)} collective-permute-done((bf16[192,640]{1,0:T(8,128)(2,1)S(1)}, bf16[192,640]{1,0:T(8,128)(2,1)S(1)}, u32[]{:S(2)}, u32[]{:S(2)}) %collective-permute-start.10) | collective-permute-done | bytes 245792 | tf_op jit(solution)/shard_map/ppermute | solution.py:182
  155.7 0.2 copy.14
  155.9 0.2 copy.15
  156.1 4.7 %collective-permute-done.12 = bf16[192,640]{1,0:T(8,128)(2,1)S(1)} collective-permute-done((bf16[192,640]{1,0:T(8,128)(2,1)S(1)}, bf16[192,640]{1,0:T(8,128)(2,1)S(1)}, u32[]{:S(2)}, u32[]{:S(2)}) %collective-permute-start.12) | collective-permute-done | bytes 245792 | tf_op jit(solution)/shard_map/ppermute | solution.py:182
  161.0 0.4 multiply_reduce_fusion
  161.5 4.6 %convert_bitcast_fusion = bf16[8,192,640]{2,1,0:T(8,128)(2,1)S(1)} fusion(bf16[192,640,1]{0,1,2:T(8,128)(2,1)S(1)} %bitcast.49, bf16[80,8,8,640]{3,2,1,0:T(8,128)(2,1)} %bitcast.60), kind=kOutput, calls=%fused_computation.5 | convolution fusion | flops 1259274240 | bytes 8765440 | tf_op jit(solution)/shard_map/qf,fkc->kqc/dot_general | solution.py:194
  166.1 31.7 %all_to_all.5 = bf16[8,192,640]{2,1,0:T(8,128)(2,1)S(1)} all-to-all(bf16[8,192,640]{2,1,0:T(8,128)(2,1)S(1)} %convert_bitcast_fusion), channel_id=1, replica_groups=mesh['place'=4,'req'=8,'tp'=8] {'tp'}, dimensions={0} | all-to-all | bytes 3932160 | tf_op jit(solution)/shard_map/all_to_all | solution.py:197
  197.7 1.0 reduce_sum.32
  (52 shorter events, 1.0 us)
Async XLA Ops:
  0.0 69.9 %copy-start = (s32[8,32]{1,0:T(8,128)S(1)}, s32[8,32]{1,0:T(8,128)}, u32[]{:S(2)}) copy-start(s32[8,32]{1,0:T(8,128)} %param.19) | copy-start | bytes 3076
  0.0 23.9 %collective-permute-start.7 = (bf16[192,640]{1,0:T(8,128)(2,1)}, bf16[192,640]{1,0:T(8,128)(2,1)S(1)}, u32[]{:S(2)}, u32[]{:S(2)}) collective-permute-start(bf16[192,640]{1,0:T(8,128)(2,1)} %q_ref.1), channel_id=1, source_target_pairs={{0,64},{8,72},{16,80},{24,88},{32,96},{40,104},{48,112},{56,120},{... | collective-permute-start | bytes 737288 | tf_op jit(solution)/shard_map/ppermute | solution.py:159
  7.2 19.9 %collective-permute-start.8 = (bf16[192,640]{1,0:T(8,128)(2,1)}, bf16[192,640]{1,0:T(8,128)(2,1)S(1)}, u32[]{:S(2)}, u32[]{:S(2)}) collective-permute-start(bf16[192,640]{1,0:T(8,128)(2,1)} %q_ref.1), channel_id=1, source_target_pairs={{0,128},{8,136},{16,144},{24,152},{32,160},{40,168},{48,176},{56,1... | collective-permute-start | bytes 737288 | tf_op jit(solution)/shard_map/ppermute | solution.py:159
  7.6 20.1 %collective-permute-start.9 = (bf16[192,640]{1,0:T(8,128)(2,1)}, bf16[192,640]{1,0:T(8,128)(2,1)}, u32[]{:S(2)}, u32[]{:S(2)}) collective-permute-start(bf16[192,640]{1,0:T(8,128)(2,1)} %q_ref.1), channel_id=1, source_target_pairs={{0,192},{8,200},{16,208},{24,216},{32,224},{40,232},{48,240},{56,2... | collective-permute-start | bytes 737288 | tf_op jit(solution)/shard_map/ppermute | solution.py:159
  13.7 35.0 %collective-permute-start.5 = (bf16[2,256,640]{2,1,0:T(8,128)(2,1)}, bf16[2,256,640]{2,1,0:T(8,128)(2,1)S(1)}, u32[]{:S(2)}, u32[]{:S(2)}) collective-permute-start(bf16[2,256,640]{2,1,0:T(8,128)(2,1)} %pad_maximum_fusion.7), channel_id=1, source_target_pairs={{0,32},{8,104},{16,48},{24,120},{32,64},{40,8},{48,80},{56,24},{64... | collective-permute-start | bytes 1966088 | tf_op jit(solution)/shard_map/ppermute | solution.py:152
  15.2 3.7 %copy-start.9 = (s32[8]{0:T(128)S(1)}, s32[8]{0:T(128)}, u32[]{:S(2)}) copy-start(s32[8]{0:T(128)} %param.16) | copy-start | bytes 100
  16.2 53.7 %collective-permute-start.6 = (bf16[2,256,640]{2,1,0:T(8,128)(2,1)}, bf16[2,256,640]{2,1,0:T(8,128)(2,1)S(1)}, u32[]{:S(2)}, u32[]{:S(2)}) collective-permute-start(bf16[2,256,640]{2,1,0:T(8,128)(2,1)} %pad_maximum_fusion.8), channel_id=1, source_target_pairs={{0,40},{8,96},{16,56},{24,112},{32,72},{40,0},{48,88},{56,16},{64,... | collective-permute-start | bytes 1966088 | tf_op jit(solution)/shard_map/ppermute | solution.py:152
  17.1 5.5 %copy-start.10 = (s32[8]{0:T(128)S(1)}, s32[8]{0:T(128)}, u32[]{:S(2)}) copy-start(s32[8]{0:T(128)} %param.18) | copy-start | bytes 100
  17.1 6.1 %copy-start.11 = (s32[8]{0:T(128)S(1)}, s32[8]{0:T(128)}, u32[]{:S(2)}) copy-start(s32[8]{0:T(128)} %param.17) | copy-start | bytes 100
  24.0 55.5 %collective-permute-start.4 = (bf16[2,256,640]{2,1,0:T(8,128)(2,1)}, bf16[2,256,640]{2,1,0:T(8,128)(2,1)S(1)}, u32[]{:S(2)}, u32[]{:S(2)}) collective-permute-start(bf16[2,256,640]{2,1,0:T(8,128)(2,1)} %pad_maximum_fusion.6), channel_id=1, source_target_pairs={{0,24},{8,16},{16,40},{24,32},{32,56},{40,48},{48,72},{56,64},{64,... | collective-permute-start | bytes 1966088 | tf_op jit(solution)/shard_map/ppermute | solution.py:152
  27.1 0.7 copy-start.7
  27.1 57.6 %collective-permute-start.3 = (bf16[2,256,640]{2,1,0:T(8,128)(2,1)}, bf16[2,256,640]{2,1,0:T(8,128)(2,1)S(1)}, u32[]{:S(2)}, u32[]{:S(2)}) collective-permute-start(bf16[2,256,640]{2,1,0:T(8,128)(2,1)} %pad_maximum_fusion.5), channel_id=1, source_target_pairs={{0,16},{8,24},{16,32},{24,40},{32,48},{40,56},{48,64},{56,72},{64,... | collective-permute-start | bytes 1966088 | tf_op jit(solution)/shard_map/ppermute | solution.py:152
  27.8 56.9 %collective-permute-start.2 = (bf16[2,256,640]{2,1,0:T(8,128)(2,1)}, bf16[2,256,640]{2,1,0:T(8,128)(2,1)S(1)}, u32[]{:S(2)}, u32[]{:S(2)}) collective-permute-start(bf16[2,256,640]{2,1,0:T(8,128)(2,1)} %pad_maximum_fusion.4), channel_id=1, source_target_pairs={{0,8},{8,0},{16,24},{24,16},{32,40},{40,32},{48,56},{56,48},{64,72... | collective-permute-start | bytes 1966088 | tf_op jit(solution)/shard_map/ppermute | solution.py:152
  48.7 37.5 %copy-start.1 = (bf16[2,256,640]{2,1,0:T(8,128)(2,1)}, bf16[2,256,640]{2,1,0:T(8,128)(2,1)S(1)}, u32[]{:S(2)}) copy-start(bf16[2,256,640]{2,1,0:T(8,128)(2,1)S(1)} %collective-permute-done.5.refs_6_) | copy-start | bytes 1966084
  48.7 36.0 %collective-permute-start.1 = (bf16[2,256,640]{2,1,0:T(8,128)(2,1)}, bf16[2,256,640]{2,1,0:T(8,128)(2,1)}, u32[]{:S(2)}, u32[]{:S(2)}) collective-permute-start(bf16[2,256,640]{2,1,0:T(8,128)(2,1)} %pad_maximum_fusion.2), channel_id=1, source_target_pairs={{0,120},{8,112},{16,8},{24,0},{32,24},{40,16},{48,40},{56,32},{64,... | collective-permute-start | bytes 1966088 | tf_op jit(solution)/shard_map/ppermute | solution.py:152
  69.8 16.3 %copy-start.2 = (bf16[2,256,640]{2,1,0:T(8,128)(2,1)}, bf16[2,256,640]{2,1,0:T(8,128)(2,1)S(1)}, u32[]{:S(2)}) copy-start(bf16[2,256,640]{2,1,0:T(8,128)(2,1)S(1)} %collective-permute-done.6.refs_7_) | copy-start | bytes 1966084
  69.8 16.3 %collective-permute-start = (bf16[2,256,640]{2,1,0:T(8,128)(2,1)}, bf16[2,256,640]{2,1,0:T(8,128)(2,1)}, u32[]{:S(2)}, u32[]{:S(2)}) collective-permute-start(bf16[2,256,640]{2,1,0:T(8,128)(2,1)} %pad_maximum_fusion.1), channel_id=1, source_target_pairs={{0,112},{8,120},{16,0},{24,8},{32,16},{40,24},{48,32},{56,40},{64,... | collective-permute-start | bytes 1966088 | tf_op jit(solution)/shard_map/ppermute | solution.py:152
  79.4 6.8 %copy-start.3 = (bf16[2,256,640]{2,1,0:T(8,128)(2,1)}, bf16[2,256,640]{2,1,0:T(8,128)(2,1)S(1)}, u32[]{:S(2)}) copy-start(bf16[2,256,640]{2,1,0:T(8,128)(2,1)S(1)} %collective-permute-done.4.refs_5_) | copy-start | bytes 1966084
  84.7 1.5 copy-start.4
  84.7 1.5 copy-start.5
  119.9 12.2 %copy-start.8 = (bf16[192,640]{1,0:T(8,128)(2,1)S(1)}, bf16[192,640]{1,0:T(8,128)(2,1)}, u32[]{:S(2)}) copy-start(bf16[192,640]{1,0:T(8,128)(2,1)} %get-tuple-element.11) | copy-start | bytes 737284
  119.9 12.4 %copy-start.6 = (bf16[576,640]{1,0:T(8,128)(2,1)S(1)}, bf16[576,640]{1,0:T(8,128)(2,1)}, u32[]{:S(2)}) copy-start(bf16[576,640]{1,0:T(8,128)(2,1)} %get-tuple-element.12) | copy-start | bytes 2211844
  123.8 15.8 %collective-permute-start.13 = (f32[192,10]{0,1:T(8,128)S(1)}, f32[192,10]{0,1:T(8,128)S(1)}, u32[]{:S(2)}, u32[]{:S(2)}) collective-permute-start(f32[192,10]{0,1:T(8,128)S(1)} %get-tuple-element.38), channel_id=1, source_target_pairs={{0,192},{8,200},{16,208},{24,216},{32,224},{40,232},{48,240},{56,2... | collective-permute-start | bytes 23048 | tf_op jit(solution)/shard_map/ppermute | solution.py:182
  130.5 9.8 %collective-permute-start.14 = (f32[192,10]{0,1:T(8,128)S(1)}, f32[192,10]{0,1:T(8,128)S(1)}, u32[]{:S(2)}, u32[]{:S(2)}) collective-permute-start(f32[192,10]{0,1:T(8,128)S(1)} %get-tuple-element.40), channel_id=1, source_target_pairs={{0,128},{8,136},{16,144},{24,152},{32,160},{40,168},{48,176},{56,1... | collective-permute-start | bytes 23048 | tf_op jit(solution)/shard_map/ppermute | solution.py:182
  132.1 8.7 %collective-permute-start.15 = (f32[192,10]{0,1:T(8,128)S(1)}, f32[192,10]{0,1:T(8,128)S(1)}, u32[]{:S(2)}, u32[]{:S(2)}) collective-permute-start(f32[192,10]{0,1:T(8,128)S(1)} %get-tuple-element.39), channel_id=1, source_target_pairs={{0,64},{8,72},{16,80},{24,88},{32,96},{40,104},{48,112},{56,120},{... | collective-permute-start | bytes 23048 | tf_op jit(solution)/shard_map/ppermute | solution.py:182
  132.4 23.3 %collective-permute-start.10 = (bf16[192,640]{1,0:T(8,128)(2,1)S(1)}, bf16[192,640]{1,0:T(8,128)(2,1)S(1)}, u32[]{:S(2)}, u32[]{:S(2)}) collective-permute-start(bf16[192,640]{1,0:T(8,128)(2,1)S(1)} %get-tuple-element.35), channel_id=1, source_target_pairs={{0,192},{8,200},{16,208},{24,216},{32,224},{40,232},{48,240},{56,2... | collective-permute-start | bytes 737288 | tf_op jit(solution)/shard_map/ppermute | solution.py:182
  139.3 16.6 %collective-permute-start.11 = (bf16[192,640]{1,0:T(8,128)(2,1)S(1)}, bf16[192,640]{1,0:T(8,128)(2,1)S(1)}, u32[]{:S(2)}, u32[]{:S(2)}) collective-permute-start(bf16[192,640]{1,0:T(8,128)(2,1)S(1)} %get-tuple-element.37), channel_id=1, source_target_pairs={{0,128},{8,136},{16,144},{24,152},{32,160},{40,168},{48,176},{56,1... | collective-permute-start | bytes 737288 | tf_op jit(solution)/shard_map/ppermute | solution.py:182
  139.7 21.2 %collective-permute-start.12 = (bf16[192,640]{1,0:T(8,128)(2,1)S(1)}, bf16[192,640]{1,0:T(8,128)(2,1)S(1)}, u32[]{:S(2)}, u32[]{:S(2)}) collective-permute-start(bf16[192,640]{1,0:T(8,128)(2,1)S(1)} %get-tuple-element.36), channel_id=1, source_target_pairs={{0,64},{8,72},{16,80},{24,88},{32,96},{40,104},{48,112},{56,120},{... | collective-permute-start | bytes 737288 | tf_op jit(solution)/shard_map/ppermute | solution.py:182
where the time goes:
time: 199 us
  waiting for transfers between devices  68.7 us (35%)
  blocking collectives  31.7 us (16%)
  Pallas kernels  31.1 us (16%)
  starting transfers between devices  30.2 us (15%)
  other arithmetic  19 us (10%)
  local copies, waits for them, and re-layouts  12.6 us (6%)
  matrix products  4.6 us (2%)
    ppermute x7, waiting for transfers between devices, layer(): chunk = lax.ppermute(chunk, seq, pairs)  48.6 us
    all_to_all x1, blocking collectives, layer(): lax.all_to_all(terms.astype(jnp.bfloat16), 'tp', split_axis=0, concat_axi...  31.7 us
    pallas_call x2, Pallas kernels, attend(): pl.pallas_call(kernel, grid_spec=pltpu.PrefetchScalarGridSpec(num_scalar_...  31.1 us
    ppermute x6, waiting for transfers between devices, layer(): got = lax.ppermute((other_sum[k - 1], other_stats[k - 1]), seq, pairs)  20.1 us
    ppermute x6, starting transfers between devices, layer(): got = lax.ppermute((other_sum[k - 1], other_stats[k - 1]), seq, pairs)  16.2 us
    ppermute x3, starting transfers between devices, layer(): span_q.append(lax.ppermute(query, seq, pairs))  8.99 us
    another operation x8, other arithmetic, layer(): jnp.stack([lax.dynamic_index_in_dim(cache_keys, sent, 0, keepdims=False),...  8.4 us
    pallas_call x4, other arithmetic, attend(): pl.pallas_call(kernel, grid_spec=pltpu.PrefetchScalarGridSpec(num_scalar_...  6.39 us
  transfers between devices with their start and end apart: 16, of which 7 were waited for; matrix products, arithmetic and copies ran while one was open for 12% of the time, Pallas kernels for 0%

commit v1 on v0

--- a/solution.py
+++ b/solution.py
@@ -194,8 +194,14 @@
     terms = jnp.einsum(
         "qf,fkc->kqc", attention, out_weight.reshape(width, parts, -1), preferred_element_type=jnp.float32
     )
-    terms = lax.all_to_all(terms.astype(jnp.bfloat16), "tp", split_axis=0, concat_axis=0, tiled=True)
-    return jnp.sum(terms.astype(jnp.float32), axis=0).astype(jnp.bfloat16)
+    terms = terms.astype(jnp.bfloat16)
+    me_tp = lax.axis_index("tp")
+    result = lax.dynamic_index_in_dim(terms, me_tp, 0, keepdims=False).astype(jnp.float32)
+    for shift in range(1, parts):
+        sent = lax.dynamic_index_in_dim(terms, (me_tp + shift) % parts, 0, keepdims=False)
+        got = lax.ppermute(sent, "tp", [(i, (i + shift) % parts) for i in range(parts)])
+        result = result + got.astype(jnp.float32)
+    return result.astype(jnp.bfloat16)
 
 
 def solution(mesh):

time: 199 us -> 201 us (1.010)
  the two profiles are of different devices: /device:TPU:8 before, /device:TPU:24 now
where the time goes in v1:
time: 201 us
  waiting for transfers between devices  86.5 us (43%)
  starting transfers between devices  43.9 us (22%)
  Pallas kernels  31.1 us (15%)
  other arithmetic  20.3 us (10%)
  local copies, waits for them, and re-layouts  13.5 us (7%)
  matrix products  4.6 us (2%)
    ppermute x7, waiting for transfers between devices, layer(): chunk = lax.ppermute(chunk, seq, pairs)  48.2 us
    pallas_call x2, Pallas kernels, attend(): pl.pallas_call(kernel, grid_spec=pltpu.PrefetchScalarGridSpec(num_scalar_...  31.1 us
    ppermute x6, waiting for transfers between devices, layer(): got = lax.ppermute((other_sum[k - 1], other_stats[k - 1]), seq, pairs)  20.1 us
    ppermute x7, waiting for transfers between devices, layer(): lax.ppermute(sent, 'tp', [(i, (i + shift) % parts) for i in range(parts)])  18.2 us
    ppermute x6, starting transfers between devices, layer(): got = lax.ppermute((other_sum[k - 1], other_stats[k - 1]), seq, pairs)  15.6 us
    ppermute x7, starting transfers between devices, layer(): lax.ppermute(sent, 'tp', [(i, (i + shift) % parts) for i in range(parts)])  13.7 us
    ppermute x3, starting transfers between devices, layer(): span_q.append(lax.ppermute(query, seq, pairs))  8.74 us
    another operation x8, other arithmetic, layer(): jnp.stack([lax.dynamic_index_in_dim(cache_keys, sent, 0, keepdims=False),...  8.38 us
  transfers between devices with their start and end apart: 23, of which 12 were waited for; matrix products, arithmetic and copies ran while one was open for 12% of the time, Pallas kernels for 0%

profile of v1, /device:TPU:24, one launch (start us, length us, event | category | flops | bytes accessed | tf_op | source)
XLA Modules:
  0.0 200.9 jit_solution(6168885380233072071)
XLA Ops:
  0.0 7.2 %collective-permute-start.7 = (bf16[192,640]{1,0:T(8,128)(2,1)}, bf16[192,640]{1,0:T(8,128)(2,1)S(1)}, u32[]{:S(2)}, u32[]{:S(2)}) collective-permute-start(bf16[192,640]{1,0:T(8,128)(2,1)} %q_ref.1), channel_id=1, source_target_pairs={{0,64},{8,72},{16,80},{24,88},{32,96},{40,104},{48,112},{56,120},{... | collective-permute-start | bytes 737288 | tf_op jit(solution)/shard_map/ppermute | solution.py:159
  7.2 0.7 collective-permute-start.8
  7.9 0.8 collective-permute-start.9
  8.7 3.8 %constant_dynamic-slice_fusion = (bf16[1,256,640]{2,1,0:T(8,128)(2,1)S(1)}, bf16[1,256,640]{2,1,0:T(8,128)(2,1)S(1)}, bf16[1,256,640]{2,1,0:T(8,128)(2,1)S(1)}, ...) fusion(bf16[8,256,640]{2,1,0:T(8,128)(2,1)} %param.14, ...), kind=kLoop, calls=%fused_computation.44 | loop fusion | bytes 10485792 | tf_op jit(solution)/shard_map/jit(dynamic_index_in_dim)/dynamic_slice | solution.py:148
  12.5 0.9 pad_maximum_fusion.7
  13.4 2.1 %collective-permute-start.5 = (bf16[2,256,640]{2,1,0:T(8,128)(2,1)}, bf16[2,256,640]{2,1,0:T(8,128)(2,1)S(1)}, u32[]{:S(2)}, u32[]{:S(2)}) collective-permute-start(bf16[2,256,640]{2,1,0:T(8,128)(2,1)} %pad_maximum_fusion.7), channel_id=1, source_target_pairs={{0,32},{8,104},{16,48},{24,120},{32,64},{40,8},{48,80},{56,24},{64... | collective-permute-start | bytes 1966088 | tf_op jit(solution)/shard_map/ppermute | solution.py:152
  15.6 0.9 pad_maximum_fusion.8
  16.5 0.9 pad_maximum_fusion.6
  17.4 0.9 pad_maximum_fusion.5
  18.3 0.9 pad_maximum_fusion.4
  19.8 0.9 pad_maximum_fusion.2
  20.7 0.9 pad_maximum_fusion.1
  24.4 2.9 %collective-permute-start.4 = (bf16[2,256,640]{2,1,0:T(8,128)(2,1)}, bf16[2,256,640]{2,1,0:T(8,128)(2,1)S(1)}, u32[]{:S(2)}, u32[]{:S(2)}) collective-permute-start(bf16[2,256,640]{2,1,0:T(8,128)(2,1)} %pad_maximum_fusion.6), channel_id=1, source_target_pairs={{0,24},{8,16},{16,40},{24,32},{32,56},{40,48},{48,72},{56,64},{64,... | collective-permute-start | bytes 1966088 | tf_op jit(solution)/shard_map/ppermute | solution.py:152
  28.5 20.5 %collective-permute-done.5.refs_6_ = bf16[2,256,640]{2,1,0:T(8,128)(2,1)S(1)} collective-permute-done((bf16[2,256,640]{2,1,0:T(8,128)(2,1)}, bf16[2,256,640]{2,1,0:T(8,128)(2,1)S(1)}, u32[]{:S(2)}, u32[]{:S(2)}) %collective-permute-start.5) | collective-permute-done | bytes 655392 | tf_op jit(solution)/shard_map/ppermute | solution.py:152
  49.0 21.2 %collective-permute-done.6.refs_7_ = bf16[2,256,640]{2,1,0:T(8,128)(2,1)S(1)} collective-permute-done((bf16[2,256,640]{2,1,0:T(8,128)(2,1)}, bf16[2,256,640]{2,1,0:T(8,128)(2,1)S(1)}, u32[]{:S(2)}, u32[]{:S(2)}) %collective-permute-start.6) | collective-permute-done | bytes 655392 | tf_op jit(solution)/shard_map/ppermute | solution.py:152
  70.8 2.5 %concatenate.35.par = s32[13]{0:T(128)} concatenate(s32[8]{0:T(128)S(1)} %broadcast_multiply_fusion, s32[1]{0:T(128)} %bitcast.11, s32[1]{0:T(128)} %dynamic_slice.71, s32[1]{0:T(128)} %dynamic_slice.72, s32[1]{0:T(128)} %dynamic_slice.73, s32[1]{0:T(128)S(1)} %bitcast.74), dimensions={0} | concatenate | bytes 104 | tf_op jit(solution)/shard_map/concatenate | solution.py:171
  73.3 2.5 %concatenate.36.par = s32[15]{0:T(128)} concatenate(s32[8]{0:T(128)S(1)} %broadcast_multiply_fusion, s32[1]{0:T(128)} %bitcast.11, s32[1]{0:T(128)} %dynamic_slice.71, s32[1]{0:T(128)} %dynamic_slice.72, s32[1]{0:T(128)} %dynamic_slice.73, s32[3]{0:T(128)S(1)} %slice.37), dimensions={0} | concatenate | bytes 120 | tf_op jit(solution)/shard_map/concatenate | solution.py:171
  75.9 2.0 pad_maximum_fusion.3.refs_2_
  77.8 2.0 %pad_maximum_fusion = bf16[3,192,640]{2,1,0:T(8,128)(2,1)} fusion(bf16[1,192,640]{2,1,0:T(8,128)(2,1)} %bitcast.15, bf16[1,192,640]{2,1,0:T(8,128)(2,1)} %bitcast.66, bf16[1,192,640]{2,1,0:T(8,128)(2,1)S(1)} %bitcast.65), kind=kLoop, calls=%fused_computation.6 | loop fusion | flops 737280 | bytes 1474560 | tf_op jit(solution)/shard_map/stack | solution.py:160
  79.9 5.1 %collective-permute-done.3.refs_4_ = bf16[2,256,640]{2,1,0:T(8,128)(2,1)S(1)} collective-permute-done((bf16[2,256,640]{2,1,0:T(8,128)(2,1)}, bf16[2,256,640]{2,1,0:T(8,128)(2,1)S(1)}, u32[]{:S(2)}, u32[]{:S(2)}) %collective-permute-start.3) | collective-permute-done | bytes 655392 | tf_op jit(solution)/shard_map/ppermute | solution.py:152
  85.0 1.4 collective-permute-done.refs_0_
  86.4 10.2 %shard_map.100 = (bf16[192,640]{1,0:T(8,128)(2,1)}, f32[5,192,1]{2,1,0:T(8,128)}, f32[5,192,1]{2,1,0:T(8,128)}) custom-call(s32[13]{0:T(128)} %concatenate.35.par, bf16[192,640]{1,0:T(8,128)(2,1)} %q_ref.1, bf16[2,256,640]{2,1,0:T(8,128)(2,1)} %collective-permute-done.refs_0_, bf16[2,256,640]{2,1,0:T(8,128)(2,1)} %collective-permute-done.1.refs_1_, ...), custom_call_target="tpu_custom_call" | custom-call | tf_op jit(solution)/shard_map/pallas_call | solution.py:79
  96.6 1.3 reduce
  97.9 1.3 reduce.1
  99.2 21.0 %shard_map.101 = (bf16[576,640]{1,0:T(8,128)(2,1)}, f32[5,576,1]{2,1,0:T(8,128)}, f32[5,576,1]{2,1,0:T(8,128)}) custom-call(s32[15]{0:T(128)} %concatenate.36.par, bf16[576,640]{1,0:T(8,128)(2,1)} %bitcast.59, bf16[2,256,640]{2,1,0:T(8,128)(2,1)} %collective-permute-done.refs_0_, bf16[2,256,640]{2,1,0:T(8,128)(2,1)} %collective-permute-done.1.refs_1_, ...), custom_call_target="tpu_custom_call" | custom-call | tf_op jit(solution)/shard_map/pallas_call | solution.py:79
  120.2 2.0 reduce.2
  122.1 1.9 reduce.3
  124.1 6.3 %collective-permute-start.13 = (f32[192,10]{0,1:T(8,128)S(1)}, f32[192,10]{0,1:T(8,128)S(1)}, u32[]{:S(2)}, u32[]{:S(2)}) collective-permute-start(f32[192,10]{0,1:T(8,128)S(1)} %get-tuple-element.45), channel_id=1, source_target_pairs={{0,192},{8,200},{16,208},{24,216},{32,224},{40,232},{48,240},{56,2... | collective-permute-start | bytes 23048 | tf_op jit(solution)/shard_map/ppermute | solution.py:182
  130.4 1.5 collective-permute-start.14
  132.1 6.9 %collective-permute-start.10 = (bf16[192,640]{1,0:T(8,128)(2,1)S(1)}, bf16[192,640]{1,0:T(8,128)(2,1)S(1)}, u32[]{:S(2)}, u32[]{:S(2)}) collective-permute-start(bf16[192,640]{1,0:T(8,128)(2,1)S(1)} %get-tuple-element.42), channel_id=1, source_target_pairs={{0,192},{8,200},{16,208},{24,216},{32,224},{40,232},{48,240},{56,2... | collective-permute-start | bytes 737288 | tf_op jit(solution)/shard_map/ppermute | solution.py:182
  140.0 3.3 %collective-permute-done.15 = f32[192,10]{0,1:T(8,128)S(1)} collective-permute-done((f32[192,10]{0,1:T(8,128)S(1)}, f32[192,10]{0,1:T(8,128)S(1)}, u32[]{:S(2)}, u32[]{:S(2)}) %collective-permute-start.15) | collective-permute-done | bytes 7712 | tf_op jit(solution)/shard_map/ppermute | solution.py:182
  143.3 12.1 %collective-permute-done.10 = bf16[192,640]{1,0:T(8,128)(2,1)S(1)} collective-permute-done((bf16[192,640]{1,0:T(8,128)(2,1)S(1)}, bf16[192,640]{1,0:T(8,128)(2,1)S(1)}, u32[]{:S(2)}, u32[]{:S(2)}) %collective-permute-start.10) | collective-permute-done | bytes 245792 | tf_op jit(solution)/shard_map/ppermute | solution.py:182
  155.8 4.7 %collective-permute-done.12 = bf16[192,640]{1,0:T(8,128)(2,1)S(1)} collective-permute-done((bf16[192,640]{1,0:T(8,128)(2,1)S(1)}, bf16[192,640]{1,0:T(8,128)(2,1)S(1)}, u32[]{:S(2)}, u32[]{:S(2)}) %collective-permute-start.12) | collective-permute-done | bytes 245792 | tf_op jit(solution)/shard_map/ppermute | solution.py:182
  161.2 4.6 %fusion.3 = bf16[192,8,640]{2,0,1:T(8,128)(2,1)S(1)} fusion(bf16[192,640,1]{0,1,2:T(8,128)(2,1)S(1)} %bitcast.64, bf16[80,8,8,640]{3,2,1,0:T(8,128)(2,1)} %bitcast.75), kind=kOutput, calls=%fused_computation.5 | convolution fusion | flops 1259274240 | bytes 8765440 | tf_op jit(solution)/shard_map/qf,fkc->kqc/dot_general | solution.py:194
  165.8 0.9 dynamic-slice_bitcast_fusion.6
  166.7 2.5 %collective-permute-start.16 = (bf16[192,640]{1,0:T(8,128)(2,1)S(1)}, bf16[192,640]{1,0:T(8,128)(2,1)S(1)}, u32[]{:S(2)}, u32[]{:S(2)}) collective-permute-start(bf16[192,640]{1,0:T(8,128)(2,1)S(1)} %get-tuple-element.35), channel_id=1, source_target_pairs={{0,1},{1,2},{2,3},{3,4},{4,5},{5,6},{6,7},{7,0},{8,9},{9,10},{10,1... | collective-permute-start | bytes 737288 | tf_op jit(solution)/shard_map/ppermute | solution.py:202
  169.2 1.5 collective-permute-start.17
  170.7 3.2 %collective-permute-start.18 = (bf16[192,640]{1,0:T(8,128)(2,1)}, bf16[192,640]{1,0:T(8,128)(2,1)}, u32[]{:S(2)}, u32[]{:S(2)}) collective-permute-start(bf16[192,640]{1,0:T(8,128)(2,1)} %get-tuple-element.40), channel_id=1, source_target_pairs={{0,3},{1,4},{2,5},{3,6},{4,7},{5,0},{6,1},{7,2},{8,11},{9,12},{10,... | collective-permute-start | bytes 737288 | tf_op jit(solution)/shard_map/ppermute | solution.py:202
  173.9 0.8 collective-permute-start.19
  174.6 2.8 %collective-permute-start.20 = (bf16[192,640]{1,0:T(8,128)(2,1)S(1)}, bf16[192,640]{1,0:T(8,128)(2,1)}, u32[]{:S(2)}, u32[]{:S(2)}) collective-permute-start(bf16[192,640]{1,0:T(8,128)(2,1)S(1)} %get-tuple-element.38), channel_id=1, source_target_pairs={{0,5},{1,6},{2,7},{3,0},{4,1},{5,2},{6,3},{7,4},{8,13},{9,14},{10,... | collective-permute-start | bytes 737288 | tf_op jit(solution)/shard_map/ppermute | solution.py:202
  177.4 1.4 collective-permute-start.21
  178.8 3.2 %collective-permute-done.17 = bf16[192,640]{1,0:T(8,128)(2,1)S(1)} collective-permute-done((bf16[192,640]{1,0:T(8,128)(2,1)S(1)}, bf16[192,640]{1,0:T(8,128)(2,1)S(1)}, u32[]{:S(2)}, u32[]{:S(2)}) %collective-permute-start.17) | collective-permute-done | bytes 245792 | tf_op jit(solution)/shard_map/ppermute | solution.py:202
  182.0 1.5 collective-permute-start.22
  183.5 2.6 %collective-permute-done.18 = bf16[192,640]{1,0:T(8,128)(2,1)} collective-permute-done((bf16[192,640]{1,0:T(8,128)(2,1)}, bf16[192,640]{1,0:T(8,128)(2,1)}, u32[]{:S(2)}, u32[]{:S(2)}) %collective-permute-start.18) | collective-permute-done | bytes 245792 | tf_op jit(solution)/shard_map/ppermute | solution.py:202
  186.2 6.5 %collective-permute-done.19 = bf16[192,640]{1,0:T(8,128)(2,1)} collective-permute-done((bf16[192,640]{1,0:T(8,128)(2,1)S(1)}, bf16[192,640]{1,0:T(8,128)(2,1)}, u32[]{:S(2)}, u32[]{:S(2)}) %collective-permute-start.19) | collective-permute-done | bytes 245792 | tf_op jit(solution)/shard_map/ppermute | solution.py:202
  192.7 3.3 %collective-permute-done.20 = bf16[192,640]{1,0:T(8,128)(2,1)} collective-permute-done((bf16[192,640]{1,0:T(8,128)(2,1)S(1)}, bf16[192,640]{1,0:T(8,128)(2,1)}, u32[]{:S(2)}, u32[]{:S(2)}) %collective-permute-start.20) | collective-permute-done | bytes 245792 | tf_op jit(solution)/shard_map/ppermute | solution.py:202
  195.9 2.6 %collective-permute-done.22 = bf16[192,640]{1,0:T(8,128)(2,1)} collective-permute-done((bf16[192,640]{1,0:T(8,128)(2,1)S(1)}, bf16[192,640]{1,0:T(8,128)(2,1)}, u32[]{:S(2)}, u32[]{:S(2)}) %collective-permute-start.22) | collective-permute-done | bytes 245792 | tf_op jit(solution)/shard_map/ppermute | solution.py:202
  198.5 2.4 %fusion.12 = bf16[192,640]{1,0:T(8,128)(2,1)} fusion(bf16[192,640]{1,0:T(8,128)(2,1)} %collective-permute-done.22, bf16[192,640]{1,0:T(8,128)(2,1)} %collective-permute-done.21, bf16[192,640]{1,0:T(8,128)(2,1)} %collective-permute-done.20, bf16[192,640]{1,0:T(8,128)(2,1)} %collective-permute-done.19, bf16[192,640]{1,0:T(8,128)(2,1)} %collective-permute-done.18, ...), kind=kLoop, calls=%fused_computation.23 | loop fusion | flops 1966080 | bytes 2211844 | tf_op jit(solution)/shard_map/convert_element_type | solution.py:204
  (66 shorter events, 6.8 us)
Async XLA Ops:
  0.0 70.1 %copy-start = (s32[8,32]{1,0:T(8,128)S(1)}, s32[8,32]{1,0:T(8,128)}, u32[]{:S(2)}) copy-start(s32[8,32]{1,0:T(8,128)} %param.19) | copy-start | bytes 3076
  0.0 24.4 %collective-permute-start.7 = (bf16[192,640]{1,0:T(8,128)(2,1)}, bf16[192,640]{1,0:T(8,128)(2,1)S(1)}, u32[]{:S(2)}, u32[]{:S(2)}) collective-permute-start(bf16[192,640]{1,0:T(8,128)(2,1)} %q_ref.1), channel_id=1, source_target_pairs={{0,64},{8,72},{16,80},{24,88},{32,96},{40,104},{48,112},{56,120},{... | collective-permute-start | bytes 737288 | tf_op jit(solution)/shard_map/ppermute | solution.py:159
  7.2 20.2 %collective-permute-start.8 = (bf16[192,640]{1,0:T(8,128)(2,1)}, bf16[192,640]{1,0:T(8,128)(2,1)S(1)}, u32[]{:S(2)}, u32[]{:S(2)}) collective-permute-start(bf16[192,640]{1,0:T(8,128)(2,1)} %q_ref.1), channel_id=1, source_target_pairs={{0,128},{8,136},{16,144},{24,152},{32,160},{40,168},{48,176},{56,1... | collective-permute-start | bytes 737288 | tf_op jit(solution)/shard_map/ppermute | solution.py:159
  7.9 20.2 %collective-permute-start.9 = (bf16[192,640]{1,0:T(8,128)(2,1)}, bf16[192,640]{1,0:T(8,128)(2,1)}, u32[]{:S(2)}, u32[]{:S(2)}) collective-permute-start(bf16[192,640]{1,0:T(8,128)(2,1)} %q_ref.1), channel_id=1, source_target_pairs={{0,192},{8,200},{16,208},{24,216},{32,224},{40,232},{48,240},{56,2... | collective-permute-start | bytes 737288 | tf_op jit(solution)/shard_map/ppermute | solution.py:159
  13.4 35.5 %collective-permute-start.5 = (bf16[2,256,640]{2,1,0:T(8,128)(2,1)}, bf16[2,256,640]{2,1,0:T(8,128)(2,1)S(1)}, u32[]{:S(2)}, u32[]{:S(2)}) collective-permute-start(bf16[2,256,640]{2,1,0:T(8,128)(2,1)} %pad_maximum_fusion.7), channel_id=1, source_target_pairs={{0,32},{8,104},{16,48},{24,120},{32,64},{40,8},{48,80},{56,24},{64... | collective-permute-start | bytes 1966088 | tf_op jit(solution)/shard_map/ppermute | solution.py:152
  15.5 3.7 %copy-start.9 = (s32[8]{0:T(128)S(1)}, s32[8]{0:T(128)}, u32[]{:S(2)}) copy-start(s32[8]{0:T(128)} %param.16) | copy-start | bytes 100
  16.5 53.7 %collective-permute-start.6 = (bf16[2,256,640]{2,1,0:T(8,128)(2,1)}, bf16[2,256,640]{2,1,0:T(8,128)(2,1)S(1)}, u32[]{:S(2)}, u32[]{:S(2)}) collective-permute-start(bf16[2,256,640]{2,1,0:T(8,128)(2,1)} %pad_maximum_fusion.8), channel_id=1, source_target_pairs={{0,40},{8,96},{16,56},{24,112},{32,72},{40,0},{48,88},{56,16},{64,... | collective-permute-start | bytes 1966088 | tf_op jit(solution)/shard_map/ppermute | solution.py:152
  17.4 5.7 %copy-start.10 = (s32[8]{0:T(128)S(1)}, s32[8]{0:T(128)}, u32[]{:S(2)}) copy-start(s32[8]{0:T(128)} %param.18) | copy-start | bytes 100
  17.4 6.3 %copy-start.11 = (s32[8]{0:T(128)S(1)}, s32[8]{0:T(128)}, u32[]{:S(2)}) copy-start(s32[8]{0:T(128)} %param.17) | copy-start | bytes 100
  24.4 55.4 %collective-permute-start.4 = (bf16[2,256,640]{2,1,0:T(8,128)(2,1)}, bf16[2,256,640]{2,1,0:T(8,128)(2,1)S(1)}, u32[]{:S(2)}, u32[]{:S(2)}) collective-permute-start(bf16[2,256,640]{2,1,0:T(8,128)(2,1)} %pad_maximum_fusion.6), channel_id=1, source_target_pairs={{0,24},{8,16},{16,40},{24,32},{32,56},{40,48},{48,72},{56,64},{64,... | collective-permute-start | bytes 1966088 | tf_op jit(solution)/shard_map/ppermute | solution.py:152
  27.4 0.7 copy-start.7
  27.4 57.6 %collective-permute-start.3 = (bf16[2,256,640]{2,1,0:T(8,128)(2,1)}, bf16[2,256,640]{2,1,0:T(8,128)(2,1)S(1)}, u32[]{:S(2)}, u32[]{:S(2)}) collective-permute-start(bf16[2,256,640]{2,1,0:T(8,128)(2,1)} %pad_maximum_fusion.5), channel_id=1, source_target_pairs={{0,16},{8,24},{16,32},{24,40},{32,48},{40,56},{48,64},{56,72},{64,... | collective-permute-start | bytes 1966088 | tf_op jit(solution)/shard_map/ppermute | solution.py:152
  28.1 56.9 %collective-permute-start.2 = (bf16[2,256,640]{2,1,0:T(8,128)(2,1)}, bf16[2,256,640]{2,1,0:T(8,128)(2,1)S(1)}, u32[]{:S(2)}, u32[]{:S(2)}) collective-permute-start(bf16[2,256,640]{2,1,0:T(8,128)(2,1)} %pad_maximum_fusion.4), channel_id=1, source_target_pairs={{0,8},{8,0},{16,24},{24,16},{32,40},{40,32},{48,56},{56,48},{64,72... | collective-permute-start | bytes 1966088 | tf_op jit(solution)/shard_map/ppermute | solution.py:152
  49.0 37.4 %copy-start.1 = (bf16[2,256,640]{2,1,0:T(8,128)(2,1)}, bf16[2,256,640]{2,1,0:T(8,128)(2,1)S(1)}, u32[]{:S(2)}) copy-start(bf16[2,256,640]{2,1,0:T(8,128)(2,1)S(1)} %collective-permute-done.5.refs_6_) | copy-start | bytes 1966084
  49.0 36.0 %collective-permute-start.1 = (bf16[2,256,640]{2,1,0:T(8,128)(2,1)}, bf16[2,256,640]{2,1,0:T(8,128)(2,1)}, u32[]{:S(2)}, u32[]{:S(2)}) collective-permute-start(bf16[2,256,640]{2,1,0:T(8,128)(2,1)} %pad_maximum_fusion.2), channel_id=1, source_target_pairs={{0,120},{8,112},{16,8},{24,0},{32,24},{40,16},{48,40},{56,32},{64,... | collective-permute-start | bytes 1966088 | tf_op jit(solution)/shard_map/ppermute | solution.py:152
  70.1 16.3 %copy-start.2 = (bf16[2,256,640]{2,1,0:T(8,128)(2,1)}, bf16[2,256,640]{2,1,0:T(8,128)(2,1)S(1)}, u32[]{:S(2)}) copy-start(bf16[2,256,640]{2,1,0:T(8,128)(2,1)S(1)} %collective-permute-done.6.refs_7_) | copy-start | bytes 1966084
  70.1 16.3 %collective-permute-start = (bf16[2,256,640]{2,1,0:T(8,128)(2,1)}, bf16[2,256,640]{2,1,0:T(8,128)(2,1)}, u32[]{:S(2)}, u32[]{:S(2)}) collective-permute-start(bf16[2,256,640]{2,1,0:T(8,128)(2,1)} %pad_maximum_fusion.1), channel_id=1, source_target_pairs={{0,112},{8,120},{16,0},{24,8},{32,16},{40,24},{48,32},{56,40},{64,... | collective-permute-start | bytes 1966088 | tf_op jit(solution)/shard_map/ppermute | solution.py:152
  79.9 6.6 %copy-start.3 = (bf16[2,256,640]{2,1,0:T(8,128)(2,1)}, bf16[2,256,640]{2,1,0:T(8,128)(2,1)S(1)}, u32[]{:S(2)}) copy-start(bf16[2,256,640]{2,1,0:T(8,128)(2,1)S(1)} %collective-permute-done.4.refs_5_) | copy-start | bytes 1966084
  85.0 1.5 copy-start.4
  85.0 1.5 copy-start.5
  120.1 11.7 %copy-start.8 = (bf16[192,640]{1,0:T(8,128)(2,1)S(1)}, bf16[192,640]{1,0:T(8,128)(2,1)}, u32[]{:S(2)}) copy-start(bf16[192,640]{1,0:T(8,128)(2,1)} %get-tuple-element.11) | copy-start | bytes 737284
  120.2 11.9 %copy-start.6 = (bf16[576,640]{1,0:T(8,128)(2,1)S(1)}, bf16[576,640]{1,0:T(8,128)(2,1)}, u32[]{:S(2)}) copy-start(bf16[576,640]{1,0:T(8,128)(2,1)} %get-tuple-element.12) | copy-start | bytes 2211844
  124.1 15.5 %collective-permute-start.13 = (f32[192,10]{0,1:T(8,128)S(1)}, f32[192,10]{0,1:T(8,128)S(1)}, u32[]{:S(2)}, u32[]{:S(2)}) collective-permute-start(f32[192,10]{0,1:T(8,128)S(1)} %get-tuple-element.45), channel_id=1, source_target_pairs={{0,192},{8,200},{16,208},{24,216},{32,224},{40,232},{48,240},{56,2... | collective-permute-start | bytes 23048 | tf_op jit(solution)/shard_map/ppermute | solution.py:182
  130.4 9.6 %collective-permute-start.14 = (f32[192,10]{0,1:T(8,128)S(1)}, f32[192,10]{0,1:T(8,128)S(1)}, u32[]{:S(2)}, u32[]{:S(2)}) collective-permute-start(f32[192,10]{0,1:T(8,128)S(1)} %get-tuple-element.47), channel_id=1, source_target_pairs={{0,128},{8,136},{16,144},{24,152},{32,160},{40,168},{48,176},{56,1... | collective-permute-start | bytes 23048 | tf_op jit(solution)/shard_map/ppermute | solution.py:182
  131.8 11.4 %collective-permute-start.15 = (f32[192,10]{0,1:T(8,128)S(1)}, f32[192,10]{0,1:T(8,128)S(1)}, u32[]{:S(2)}, u32[]{:S(2)}) collective-permute-start(f32[192,10]{0,1:T(8,128)S(1)} %get-tuple-element.46), channel_id=1, source_target_pairs={{0,64},{8,72},{16,80},{24,88},{32,96},{40,104},{48,112},{56,120},{... | collective-permute-start | bytes 23048 | tf_op jit(solution)/shard_map/ppermute | solution.py:182
  132.1 23.3 %collective-permute-start.10 = (bf16[192,640]{1,0:T(8,128)(2,1)S(1)}, bf16[192,640]{1,0:T(8,128)(2,1)S(1)}, u32[]{:S(2)}, u32[]{:S(2)}) collective-permute-start(bf16[192,640]{1,0:T(8,128)(2,1)S(1)} %get-tuple-element.42), channel_id=1, source_target_pairs={{0,192},{8,200},{16,208},{24,216},{32,224},{40,232},{48,240},{56,2... | collective-permute-start | bytes 737288 | tf_op jit(solution)/shard_map/ppermute | solution.py:182
  139.0 16.6 %collective-permute-start.11 = (bf16[192,640]{1,0:T(8,128)(2,1)S(1)}, bf16[192,640]{1,0:T(8,128)(2,1)S(1)}, u32[]{:S(2)}, u32[]{:S(2)}) collective-permute-start(bf16[192,640]{1,0:T(8,128)(2,1)S(1)} %get-tuple-element.44), channel_id=1, source_target_pairs={{0,128},{8,136},{16,144},{24,152},{32,160},{40,168},{48,176},{56,1... | collective-permute-start | bytes 737288 | tf_op jit(solution)/shard_map/ppermute | solution.py:182
  139.6 21.0 %collective-permute-start.12 = (bf16[192,640]{1,0:T(8,128)(2,1)S(1)}, bf16[192,640]{1,0:T(8,128)(2,1)S(1)}, u32[]{:S(2)}, u32[]{:S(2)}) collective-permute-start(bf16[192,640]{1,0:T(8,128)(2,1)S(1)} %get-tuple-element.43), channel_id=1, source_target_pairs={{0,64},{8,72},{16,80},{24,88},{32,96},{40,104},{48,112},{56,120},{... | collective-permute-start | bytes 737288 | tf_op jit(solution)/shard_map/ppermute | solution.py:182
  166.7 10.8 %collective-permute-start.16 = (bf16[192,640]{1,0:T(8,128)(2,1)S(1)}, bf16[192,640]{1,0:T(8,128)(2,1)S(1)}, u32[]{:S(2)}, u32[]{:S(2)}) collective-permute-start(bf16[192,640]{1,0:T(8,128)(2,1)S(1)} %get-tuple-element.35), channel_id=1, source_target_pairs={{0,1},{1,2},{2,3},{3,4},{4,5},{5,6},{6,7},{7,0},{8,9},{9,10},{10,1... | collective-permute-start | bytes 737288 | tf_op jit(solution)/shard_map/ppermute | solution.py:202
  169.2 12.9 %collective-permute-start.17 = (bf16[192,640]{1,0:T(8,128)(2,1)S(1)}, bf16[192,640]{1,0:T(8,128)(2,1)S(1)}, u32[]{:S(2)}, u32[]{:S(2)}) collective-permute-start(bf16[192,640]{1,0:T(8,128)(2,1)S(1)} %get-tuple-element.41), channel_id=1, source_target_pairs={{0,2},{1,3},{2,4},{3,5},{4,6},{5,7},{6,0},{7,1},{8,10},{9,11},{10,... | collective-permute-start | bytes 737288 | tf_op jit(solution)/shard_map/ppermute | solution.py:202
  170.7 15.5 %collective-permute-start.18 = (bf16[192,640]{1,0:T(8,128)(2,1)}, bf16[192,640]{1,0:T(8,128)(2,1)}, u32[]{:S(2)}, u32[]{:S(2)}) collective-permute-start(bf16[192,640]{1,0:T(8,128)(2,1)} %get-tuple-element.40), channel_id=1, source_target_pairs={{0,3},{1,4},{2,5},{3,6},{4,7},{5,0},{6,1},{7,2},{8,11},{9,12},{10,... | collective-permute-start | bytes 737288 | tf_op jit(solution)/shard_map/ppermute | solution.py:202
  173.9 18.8 %collective-permute-start.19 = (bf16[192,640]{1,0:T(8,128)(2,1)S(1)}, bf16[192,640]{1,0:T(8,128)(2,1)}, u32[]{:S(2)}, u32[]{:S(2)}) collective-permute-start(bf16[192,640]{1,0:T(8,128)(2,1)S(1)} %get-tuple-element.39), channel_id=1, source_target_pairs={{0,4},{1,5},{2,6},{3,7},{4,0},{5,1},{6,2},{7,3},{8,12},{9,13},{10,... | collective-permute-start | bytes 737288 | tf_op jit(solution)/shard_map/ppermute | solution.py:202
  174.6 21.3 %collective-permute-start.20 = (bf16[192,640]{1,0:T(8,128)(2,1)S(1)}, bf16[192,640]{1,0:T(8,128)(2,1)}, u32[]{:S(2)}, u32[]{:S(2)}) collective-permute-start(bf16[192,640]{1,0:T(8,128)(2,1)S(1)} %get-tuple-element.38), channel_id=1, source_target_pairs={{0,5},{1,6},{2,7},{3,0},{4,1},{5,2},{6,3},{7,4},{8,13},{9,14},{10,... | collective-permute-start | bytes 737288 | tf_op jit(solution)/shard_map/ppermute | solution.py:202
  177.4 18.5 %collective-permute-start.21 = (bf16[192,640]{1,0:T(8,128)(2,1)S(1)}, bf16[192,640]{1,0:T(8,128)(2,1)}, u32[]{:S(2)}, u32[]{:S(2)}) collective-permute-start(bf16[192,640]{1,0:T(8,128)(2,1)S(1)} %get-tuple-element.37), channel_id=1, source_target_pairs={{0,6},{1,7},{2,0},{3,1},{4,2},{5,3},{6,4},{7,5},{8,14},{9,15},{10,... | collective-permute-start | bytes 737288 | tf_op jit(solution)/shard_map/ppermute | solution.py:202
  182.0 16.5 %collective-permute-start.22 = (bf16[192,640]{1,0:T(8,128)(2,1)S(1)}, bf16[192,640]{1,0:T(8,128)(2,1)}, u32[]{:S(2)}, u32[]{:S(2)}) collective-permute-start(bf16[192,640]{1,0:T(8,128)(2,1)S(1)} %get-tuple-element.36), channel_id=1, source_target_pairs={{0,7},{1,0},{2,1},{3,2},{4,3},{5,4},{6,5},{7,6},{8,15},{9,8},{10,9... | collective-permute-start | bytes 737288 | tf_op jit(solution)/shard_map/ppermute | solution.py:202
